TPU v7x, 128 devices: a whole 4x4x4 slice. The times are simulated.
128 devices in a mesh: expert: 32 (over y, x, core), dp: 4 (over z).
Axes of the slice: x: 4, y: 4, z: 4, core: 2. Of those that a mesh axis runs over, the one named last changes fastest.
Arguments:
- tokens: bfloat16 [4096, 4096], P('expert', 'dp'), may hold values from -6 to 6
- cotangent: bfloat16 [4096, 4096], P('expert', 'dp'), may hold values from -6 to 6
- gate_probs: bfloat16 [4096, 8], P('expert'), may hold values from 0.019897461 to 0.3984375
- expert_ids: int32 [4096, 8], P('expert'), may hold values from 0 to 31, all different within a row; in each aligned block of 128 rows (0 to 127, 128 to 255, ...) at most 36 rows name the same one
- gate_weight: bfloat16 [32, 4096, 1024], P('expert', 'dp'), may hold values from -0.09375 to 0.09375
- up_weight: bfloat16 [32, 4096, 1024], P('expert', 'dp'), may hold values from -0.09375 to 0.09375
- down_weight: bfloat16 [32, 1024, 4096], P('expert', None, 'dp'), may hold values from -0.1875 to 0.1875
Outputs:
- grad_tokens: bfloat16 [4096, 4096], P('expert', 'dp')
- grad_gates: float32 [4096, 8], P('expert')
- grad_gate_weight: float32 [32, 4096, 1024], P('expert', 'dp')
- grad_up_weight: float32 [32, 4096, 1024], P('expert', 'dp')
- grad_down_weight: float32 [32, 1024, 4096], P('expert', None, 'dp')
Inputs may be any that keep to these rules, and one draw needn't show every extreme that they name: `expert_ids`: each row names 8 different experts. Among the 128 rows of one group no expert is named more than 36 times, and in every draw some expert is named exactly 36 times by the rows of some group.
All inputs are finite; a program needn't handle non-finite values.
Results may differ from a plain program's by a relative error of at most 0.012.
Values may be sent and summed in bfloat16 or wider, within the bound.
A program may use at most 128 MiB of HBM per device.

v0:
```python
import jax
import jax.numpy as jnp
from jax import lax
from jax.sharding import PartitionSpec as P

TOP = 8
EXPERTS = 32
CAP = 36


def local_slots(expert_ids):
    flat_ids = expert_ids.reshape(-1)
    columns = jnp.arange(EXPERTS, dtype=jnp.int32)
    member = (flat_ids[:, None] == columns[None, :]).astype(jnp.int32)
    ranked = jnp.cumsum(member, axis=0) - 1
    within = jnp.sum(member * ranked, axis=1)
    return flat_ids * CAP + within


def pack_rows(tokens, cotangent, gate_probs, target):
    token_count = tokens.shape[0]
    slot_total = EXPERTS * CAP
    slot_index = jnp.arange(slot_total, dtype=jnp.int32)
    placed = target[None, :] == slot_index[:, None]
    chosen = jnp.any(placed.reshape(slot_total, token_count, TOP), axis=2).astype(jnp.bfloat16)
    x_send = jnp.dot(chosen, tokens, preferred_element_type=jnp.float32).astype(jnp.bfloat16)
    dy_send = jnp.dot(chosen, cotangent, preferred_element_type=jnp.float32).astype(jnp.bfloat16)
    weights_flat = gate_probs.reshape(-1).astype(jnp.float32)
    g_send = jnp.sum(jnp.where(placed, weights_flat[None, :], 0.0), axis=1).astype(jnp.bfloat16)
    return (x_send, dy_send, g_send)


def hidden_units(gate_pre, up_pre, back_hidden, g_rows):
    sigmoid_gate = jax.nn.sigmoid(gate_pre)
    swish_gate = gate_pre * sigmoid_gate
    hidden = (swish_gate * up_pre).astype(jnp.bfloat16)
    product = back_hidden * hidden.astype(jnp.float32)
    grad_hidden = g_rows * back_hidden
    derivative = sigmoid_gate * (1.0 + gate_pre * (1.0 - sigmoid_gate))
    grad_gate_pre = (grad_hidden * up_pre * derivative).astype(jnp.bfloat16)
    grad_up_pre = (grad_hidden * swish_gate).astype(jnp.bfloat16)
    return (hidden, grad_gate_pre, grad_up_pre, product)


def shards(tokens, cotangent, gate_probs, expert_ids, gate_weight, up_weight, down_weight):
    expert_count = lax.axis_size("expert")
    data_count = lax.axis_size("dp")
    local_count = gate_weight.shape[0]
    width_part = tokens.shape[1]
    token_count = tokens.shape[0]
    target = local_slots(expert_ids)
    x_send, dy_send, g_send = pack_rows(tokens, cotangent, gate_probs, target)
    x_recv, dy_recv, g_recv = (
        lax.all_to_all(x_send, "expert", split_axis=0, concat_axis=0, tiled=True),
        lax.all_to_all(dy_send, "expert", split_axis=0, concat_axis=0, tiled=True),
        lax.all_to_all(g_send, "expert", split_axis=0, concat_axis=0, tiled=True),
    )
    x_grid = x_recv.reshape(expert_count, local_count, CAP, width_part)
    dy_grid = dy_recv.reshape(expert_count, local_count, CAP, width_part)
    g_grid = g_recv.reshape(expert_count, local_count, CAP)
    g_rows = jnp.transpose(g_grid, (1, 0, 2)).astype(jnp.float32)[..., None]
    gate_part = jnp.einsum(
        "secd,edf->escf", x_grid, gate_weight, preferred_element_type=jnp.float32
    )
    up_part = jnp.einsum("secd,edf->escf", x_grid, up_weight, preferred_element_type=jnp.float32)
    back_part = jnp.einsum(
        "secd,efd->escf", dy_grid, down_weight, preferred_element_type=jnp.float32
    )
    gate_pre, up_pre, back_hidden = (
        lax.psum_scatter(gate_part, "dp", scatter_dimension=3, tiled=True),
        lax.psum_scatter(up_part, "dp", scatter_dimension=3, tiled=True),
        lax.psum_scatter(back_part, "dp", scatter_dimension=3, tiled=True),
    )
    hidden, grad_gate_pre, grad_up_pre, product = hidden_units(
        gate_pre, up_pre, back_hidden, g_rows
    )
    block_sum = jnp.sum(product, axis=3, keepdims=True).astype(jnp.bfloat16)
    hidden_all, gate_grad_all, up_grad_all, gate_blocks = (
        lax.all_gather(hidden, "dp", axis=3, tiled=True),
        lax.all_gather(grad_gate_pre, "dp", axis=3, tiled=True),
        lax.all_gather(grad_up_pre, "dp", axis=3, tiled=True),
        lax.all_gather(block_sum, "dp", axis=3, tiled=True),
    )
    input_terms = jnp.einsum(
        "escf,edf->secd", gate_grad_all, gate_weight, preferred_element_type=jnp.float32
    )
    input_terms = input_terms + jnp.einsum(
        "escf,edf->secd", up_grad_all, up_weight, preferred_element_type=jnp.float32
    )
    input_part = input_terms.astype(jnp.bfloat16).reshape(
        expert_count * local_count * CAP, width_part
    )
    scaled_dy = dy_grid * g_grid[..., None]
    grad_down = jnp.einsum(
        "escf,secd->efd", hidden_all, scaled_dy, preferred_element_type=jnp.float32
    )
    grad_gate = jnp.einsum(
        "secd,escf->edf", x_grid, gate_grad_all, preferred_element_type=jnp.float32
    )
    grad_up = jnp.einsum("secd,escf->edf", x_grid, up_grad_all, preferred_element_type=jnp.float32)
    block_send = jnp.transpose(gate_blocks, (1, 0, 2, 3)).reshape(
        expert_count * local_count * CAP, data_count
    )
    input_table, gate_table = (
        lax.all_to_all(input_part, "expert", split_axis=0, concat_axis=0, tiled=True),
        lax.all_to_all(block_send, "expert", split_axis=0, concat_axis=0, tiled=True),
    )
    picked = jnp.take(input_table, target, axis=0).astype(jnp.float32)
    grad_tokens = picked.reshape(token_count, TOP, width_part).sum(1).astype(jnp.bfloat16)
    grad_gates = (
        jnp.take(gate_table, target, axis=0).astype(jnp.float32).sum(1).reshape(token_count, TOP)
    )
    return (grad_tokens, grad_gates, grad_gate, grad_up, grad_down)


def solution(mesh):
    placed = (
        P("expert", "dp"),
        P("expert", "dp"),
        P("expert", None),
        P("expert", None),
        P("expert", "dp", None),
        P("expert", "dp", None),
        P("expert", None, "dp"),
    )
    return jax.shard_map(
        shards,
        mesh=mesh,
        in_specs=placed,
        out_specs=(
            P("expert", "dp"),
            P("expert", None),
            P("expert", "dp", None),
            P("expert", "dp", None),
            P("expert", None, "dp"),
        ),
        check_vma=False,
    )
```

profile of v0, /device:TPU:0, one launch (start us, length us, event | category | flops | bytes accessed | tf_op | source)
XLA Modules:
  0.0 406.6 jit_solution(17590556254104163297)
XLA Ops:
  8.4 9.0 %reduce-window.6 = s32[32,8,128]{2,1,0:T(8,128)S(1)} reduce-window(s32[32,8,128]{2,1,0:T(8,128)S(1)} %fusion.37, s32[]{:T(128)} %constant.25.clone.1), window={size=1x1x128 pad=0_0x0_0x127_0}, to_apply=%region_0.0 | reduce-window | flops 4161536 | bytes 262148 | tf_op jit(solution)/shard_map/reduce-window
  18.7 4.2 %fusion = pred[1152,128]{1,0:T(8,128)(4,1)S(1)} fusion(s32[128,8]{0,1:T(8,128)S(1)} %get-tuple-element.35), kind=kLoop, calls=%fused_computation.6 | loop fusion | flops 2211840 | bytes 151552 | tf_op jit(solution)/shard_map/reduce_or | solution.py:25
  30.1 41.6 %all_to_all.45 = bf16[32,36,1024]{2,1,0:T(8,128)(2,1)S(1)} all-to-all(bf16[32,36,1024]{2,1,0:T(8,128)(2,1)} %all_to_all.33), channel_id=1, replica_groups=mesh['expert'=32,'dp'=4] {'expert'}, dimensions={0} | all-to-all | bytes 4718592 | tf_op jit(solution)/shard_map/all_to_all | solution.py:54
  73.2 4.6 %convolution_bitcast_fusion.1 = f32[1,32,36,1024]{3,2,1,0:T(8,128)} fusion(bf16[32,36,1024]{2,1,0:T(8,128)(2,1)S(1)} %all_to_all.45, bf16[1,1024,1024]{2,1,0:T(8,128)(2,1)S(1)} %copy-done), kind=kOutput, calls=%fused_computation.21 | convolution fusion | flops 2415919104 | bytes 9175040 | tf_op jit(solution)/shard_map/secd,edf->escf/dot_general | solution.py:65
  77.9 7.6 %convolution_bitcast_fusion = f32[1,32,36,1024]{3,2,1,0:T(8,128)} fusion(bf16[32,36,1024]{2,1,0:T(8,128)(2,1)} %copy-done.2, bf16[1,1024,1024]{2,1,0:T(8,128)(2,1)} %param.11), kind=kOutput, calls=%fused_computation.20 | convolution fusion | flops 2415919104 | bytes 9175040 | tf_op jit(solution)/shard_map/secd,edf->escf/dot_general | solution.py:62
  92.8 38.4 %all_to_all.46 = bf16[32,36,1024]{2,1,0:T(8,128)(2,1)S(1)} all-to-all(bf16[32,36,1024]{2,1,0:T(8,128)(2,1)} %all_to_all.31), channel_id=1, replica_groups=mesh['expert'=32,'dp'=4] {'expert'}, dimensions={0} | all-to-all | bytes 4718592 | tf_op jit(solution)/shard_map/all_to_all | solution.py:55
  132.7 4.7 %convolution_bitcast_fusion.2 = f32[1,32,36,1024]{3,2,1,0:T(8,128)} fusion(bf16[32,36,1024]{2,1,0:T(8,128)(2,1)S(1)} %all_to_all.46, bf16[1,1024,1024]{2,1,0:T(8,128)(2,1)S(1)} %copy-done.9), kind=kOutput, calls=%fused_computation.22 | convolution fusion | flops 2415919104 | bytes 9175040 | tf_op jit(solution)/shard_map/secd,efd->escf/dot_general | solution.py:66
  139.0 10.7 %all_to_all.47 = bf16[32,36,1]{1,2,0:T(2,128)(2,1)S(1)} all-to-all(bf16[32,36,1]{1,2,0:T(2,128)(2,1)S(1)} %convert_element_type.99), channel_id=1, replica_groups=mesh['expert'=32,'dp'=4] {'expert'}, dimensions={0} | all-to-all | bytes 4608 | tf_op jit(solution)/shard_map/all_to_all | solution.py:56
  149.7 40.1 %reduce-scatter.8.cloned.1.call-done = f32[1,32,36,256]{3,2,1,0:T(8,128)} async-done(((f32[1,32,36,1024]{3,2,1,0:T(8,128)}), f32[1,32,36,256]{3,2,1,0:T(8,128)}) %reduce-scatter.8.cloned.1.call-update) | async-done | bytes 1179664 | tf_op jit(solution)/shard_map/reduce_scatter | solution.py:70
  189.9 57.6 %reduce-scatter.4.cloned.1.call-done = f32[1,32,36,256]{3,2,1,0:T(8,128)} async-done(((f32[1,32,36,1024]{3,2,1,0:T(8,128)}), f32[1,32,36,256]{3,2,1,0:T(8,128)}) %reduce-scatter.4.cloned.1.call-update) | async-done | bytes 1179664 | tf_op jit(solution)/shard_map/reduce_scatter | solution.py:72
  247.5 4.3 %multiply_reduce_fusion = (bf16[32,36]{1,0:T(8,128)(2,1)S(1)}, bf16[1,32,36,256]{3,2,1,0:T(8,128)(2,1)}, bf16[1,32,36,256]{3,2,1,0:T(8,128)(2,1)}, bf16[1,32,36,256]{3,2,1,0:T(8,128)(2,1)}) fusion(f32[1,32,36,256]{3,2,1,0:T(8,128)} %reduce-scatter.4.cloned.1.call-done, f32[1,32,36,256]{3,2,1,0:T(8,128)} %reduce-scatter.6.cloned.1.call-done, ...), kind=kLoop, calls=%fused_computation.34 | loop fusion | flops 5602176 | bytes 5315328 | tf_op jit(solution)/shard_map/reduce_sum | solution.py:77
  252.6 11.9 %all_gather.14 = bf16[1,32,36,4]{2,1,0,3:T(8,128)(2,1)S(1)} all-gather(bf16[1,32,36,1]{2,1,0,3:T(8,128)(2,1)S(1)} %bitcast.97), channel_id=1, replica_groups=mesh['expert'=32,'dp'=4] {'dp'}, dimensions={3}, use_global_device_ids=true | all-gather | bytes 11520 | tf_op jit(solution)/shard_map/all_gather | solution.py:82
  265.2 7.1 %all-to-all-start.4 = ((bf16[32,36,4]{1,2,0:T(4,128)(2,1)}), bf16[32,36,4]{1,2,0:T(4,128)(2,1)S(1)}, u32[]{:S(2)}, u32[]{:S(2)}) async-start(bf16[32,36,4]{1,2,0:T(4,128)(2,1)} %copy.68), calls=%async_computation.7 | async-start | bytes 65536 | tf_op jit(solution)/shard_map/all_to_all | solution.py:106
  272.9 6.8 %all-to-all-done.4 = bf16[32,36,4]{1,2,0:T(4,128)(2,1)S(1)} async-done(((bf16[32,36,4]{1,2,0:T(4,128)(2,1)}), bf16[32,36,4]{1,2,0:T(4,128)(2,1)S(1)}, u32[]{:S(2)}, u32[]{:S(2)}) %all-to-all-start.4) | async-done | bytes 9248 | tf_op jit(solution)/shard_map/all_to_all | solution.py:106
  284.4 6.2 %all-gather.6.cloned.1.call-done = bf16[1,32,36,1024]{3,2,1,0:T(8,128)(2,1)} async-done(((bf16[1,32,36,256]{3,2,1,0:T(8,128)(2,1)}), bf16[1,32,36,1024]{3,2,1,0:T(8,128)(2,1)}) %all-gather.6.cloned.1.call-update) | async-done | bytes 2359312 | tf_op jit(solution)/shard_map/all_gather | solution.py:81
  290.6 6.4 %fusion.5 = f32[32,36,1024]{2,1,0:T(8,128)} fusion(bf16[1,32,36,1024]{3,2,1,0:T(8,128)(2,1)} %all-gather.6.cloned.1.call-done, bf16[1,1024,1024]{2,1,0:T(8,128)(2,1)S(1)} %copy-done), kind=kOutput, calls=%fused_computation.13 | convolution fusion | flops 2415919104 | bytes 9175040 | tf_op jit(solution)/shard_map/escf,edf->secd/dot_general | solution.py:87
  297.0 35.6 %all-gather.4.cloned.1.call-done = bf16[1,32,36,1024]{3,2,1,0:T(8,128)(2,1)} async-done(((bf16[1,32,36,256]{3,2,1,0:T(8,128)(2,1)}), bf16[1,32,36,1024]{3,2,1,0:T(8,128)(2,1)}) %all-gather.4.cloned.1.call-update) | async-done | bytes 2359312 | tf_op jit(solution)/shard_map/all_gather | solution.py:80
  332.6 8.3 %add_convert_fusion = bf16[32,36,1024]{2,1,0:T(8,128)(2,1)} fusion(f32[32,36,1024]{2,1,0:T(8,128)} %fusion.5, bf16[1,1024,1024]{2,1,0:T(8,128)(2,1)} %param.11, bf16[1,32,36,1024]{3,2,1,0:T(8,128)(2,1)} %all-gather.4.cloned.1.call-done), kind=kOutput, calls=%fused_computation.2 | convolution fusion | flops 2418278400 | bytes 11534336 | tf_op jit(solution)/shard_map/escf,edf->secd/dot_general | solution.py:84
  340.9 7.4 %all-to-all-start.3 = ((bf16[32,36,1024]{2,1,0:T(8,128)(2,1)}), bf16[32,36,1024]{2,1,0:T(8,128)(2,1)}, u32[]{:S(2)}, u32[]{:S(2)}) async-start(bf16[32,36,1024]{2,1,0:T(8,128)(2,1)} %add_convert_fusion), calls=%async_computation.6 | async-start | bytes 5242880 | tf_op jit(solution)/shard_map/all_to_all | solution.py:105
  348.4 7.7 %fusion.12 = f32[1,1024,1024]{2,1,0:T(8,128)} fusion(bf16[32,36,1024]{2,1,0:T(8,128)(2,1)} %copy-done.2, bf16[1,32,36,1024]{3,2,1,0:T(8,128)(2,1)} %all-gather.4.cloned.1.call-done), kind=kOutput, calls=%fused_computation.23 | convolution fusion | flops 2415919104 | bytes 8912896 | tf_op jit(solution)/shard_map/secd,escf->edf/dot_general | solution.py:97
  356.0 4.5 %fusion.15 = f32[1,1024,1024]{2,1,0:T(8,128)} fusion(bf16[32,36,1024]{2,1,0:T(8,128)(2,1)S(1)} %copy-done.3, bf16[1,32,36,1024]{3,2,1,0:T(8,128)(2,1)S(1)} %copy-done.8), kind=kOutput, calls=%fused_computation.24 | convolution fusion | flops 2415919104 | bytes 8912896 | tf_op jit(solution)/shard_map/secd,escf->edf/dot_general | solution.py:100
  360.5 14.1 %all-gather.8.cloned.1.call-done = bf16[1,32,36,1024]{3,2,1,0:T(8,128)(2,1)} async-done(((bf16[1,32,36,256]{3,2,1,0:T(8,128)(2,1)}), bf16[1,32,36,1024]{3,2,1,0:T(8,128)(2,1)}) %all-gather.8.cloned.1.call-update) | async-done | bytes 2359312 | tf_op jit(solution)/shard_map/all_gather | solution.py:79
  374.6 7.5 %fusion.18 = f32[1,1024,1024]{2,1,0:T(8,128)} fusion(bf16[32,36,1024]{2,1,0:T(8,128)(2,1)} %copy-done.4, bf16[1,32,36,1024]{3,2,1,0:T(8,128)(2,1)} %all-gather.8.cloned.1.call-done, bf16[32,36]{1,0:T(8,128)(2,1)S(1)} %get-tuple-element.37), kind=kOutput, calls=%fused_computation.25 | convolution fusion | flops 2417098752 | bytes 8915200 | tf_op jit(solution)/shard_map/escf,secd->efd/dot_general | solution.py:94
  388.2 8.1 %gather_fusion = bf16[1024,1024]{1,0:T(8,128)(2,1)} fusion(bf16[1152,1024]{1,0:T(8,128)(2,1)} %all_to_all.36, s32[1024]{0:T(1024)S(1)} %broadcast_clamp_fusion), kind=kCustom, calls=%fused_computation | custom fusion | bytes 4198400 | tf_op jit(solution)/shard_map/jit(_take)/gather | solution.py:108
  (74 shorter events, 37.7 us)
Async XLA Ops:
  7.2 66.1 %copy-start = (bf16[1,1024,1024]{2,1,0:T(8,128)(2,1)S(1)}, bf16[1,1024,1024]{2,1,0:T(8,128)(2,1)}, u32[]{:S(2)}) copy-start(bf16[1,1024,1024]{2,1,0:T(8,128)(2,1)} %param.12) | copy-start | bytes 6291460
  7.2 142.6 %reduce-scatter.6.cloned.1.call-start = ((), (), s32[]{:S(2)}) async-start(), calls=%async_computation.9 | async-start | bytes 6553600 | tf_op jit(solution)/shard_map/reduce_scatter | solution.py:71
  71.7 1.5 copy-start.2
  77.9 112.0 %reduce-scatter.8.cloned.1.call-start = ((), (), s32[]{:S(2)}) async-start(), calls=%async_computation.10 | async-start | bytes 6553600 | tf_op jit(solution)/shard_map/reduce_scatter | solution.py:70
  85.5 1.0 copy-start.5
  85.5 162.0 %reduce-scatter.4.cloned.1.call-start = ((), (), s32[]{:S(2)}) async-start(), calls=%async_computation.8 | async-start | bytes 6553600 | tf_op jit(solution)/shard_map/reduce_scatter | solution.py:72
  92.8 39.9 %copy-start.9 = (bf16[1,1024,1024]{2,1,0:T(8,128)(2,1)S(1)}, bf16[1,1024,1024]{2,1,0:T(8,128)(2,1)}, u32[]{:S(2)}) copy-start(bf16[1,1024,1024]{2,1,0:T(8,128)(2,1)} %param.13) | copy-start | bytes 6291460
  131.2 1.5 copy-start.4
  137.4 0.7 copy-start.7
  137.4 153.2 %all-gather.6.cloned.1.call-start = ((), (), s32[]{:S(2)}) async-start(), calls=%async_computation.12 | async-start | bytes 3276800 | tf_op jit(solution)/shard_map/all_gather | solution.py:81
  247.5 4.9 %copy-start.6 = (s32[128,8]{0,1:T(8,128)S(1)}, s32[128,8]{0,1:T(8,128)}, u32[]{:S(2)}) copy-start(s32[128,8]{0,1:T(8,128)} %param.10) | copy-start | bytes 12292
  251.8 80.8 %all-gather.4.cloned.1.call-start = ((), (), s32[]{:S(2)}) async-start(), calls=%async_computation.11 | async-start | bytes 3276800 | tf_op jit(solution)/shard_map/all_gather | solution.py:80
  265.2 14.5 %all-to-all-start.4 = ((bf16[32,36,4]{1,2,0:T(4,128)(2,1)}), bf16[32,36,4]{1,2,0:T(4,128)(2,1)S(1)}, u32[]{:S(2)}, u32[]{:S(2)}) async-start(bf16[32,36,4]{1,2,0:T(4,128)(2,1)} %copy.68), calls=%async_computation.7 | async-start | bytes 65536 | tf_op jit(solution)/shard_map/all_to_all | solution.py:106
  272.3 102.3 %all-gather.8.cloned.1.call-start = ((), (), s32[]{:S(2)}) async-start(), calls=%async_computation.13 | async-start | bytes 3276800 | tf_op jit(solution)/shard_map/all_gather | solution.py:79
  340.9 43.2 %all-to-all-start.3 = ((bf16[32,36,1024]{2,1,0:T(8,128)(2,1)}), bf16[32,36,1024]{2,1,0:T(8,128)(2,1)}, u32[]{:S(2)}, u32[]{:S(2)}) async-start(bf16[32,36,1024]{2,1,0:T(8,128)(2,1)} %add_convert_fusion), calls=%async_computation.6 | async-start | bytes 5242880 | tf_op jit(solution)/shard_map/all_to_all | solution.py:105
  348.3 7.7 %copy-start.3 = (bf16[32,36,1024]{2,1,0:T(8,128)(2,1)S(1)}, bf16[32,36,1024]{2,1,0:T(8,128)(2,1)}, u32[]{:S(2)}) copy-start(bf16[32,36,1024]{2,1,0:T(8,128)(2,1)} %copy-done.2) | copy-start | bytes 7077892
  348.4 7.7 %copy-start.8 = (bf16[1,32,36,1024]{3,2,1,0:T(8,128)(2,1)S(1)}, bf16[1,32,36,1024]{3,2,1,0:T(8,128)(2,1)}, u32[]{:S(2)}) copy-start(bf16[1,32,36,1024]{3,2,1,0:T(8,128)(2,1)} %all-gather.6.cloned.1.call-done) | copy-start | bytes 7077892
  388.2 11.5 %copy-start.1 = (bf16[1,1024,1024]{2,1,0:T(8,128)(2,1)S(1)}, bf16[1,1024,1024]{2,1,0:T(8,128)(2,1)}, u32[]{:S(2)}) copy-start(bf16[1,1024,1024]{2,1,0:T(8,128)(2,1)} %param.12) | copy-start | bytes 6291460
Sparse Core Ops, SparseCore 0:
  78.0 54.2 reduce-scatter.5
  134.7 55.1 reduce-scatter.7
  192.3 55.1 reduce-scatter.3
  251.9 38.6 all-gather.5
  292.7 39.8 all-gather.3
  334.7 39.8 all-gather.7
where the time goes:
time: 408 us; the launch traced here: 407 us
  waiting for transfers between devices  163 us (40%)
  blocking collectives  103 us (25%)
  matrix products  56.6 us (14%)
  local copies, waits for them, and re-layouts  32.1 us (8%)
  other arithmetic  22.7 us (6%)
  starting transfers between devices  14.8 us (4%)
  between operations  14.3 us (4%)
    reduce_scatter x1, waiting for transfers between devices, shards(): lax.psum_scatter(back_part, 'dp', scatter_dimension=3, tiled=True)  57.6 us
    all_to_all x1, blocking collectives, shards(): lax.all_to_all(x_send, 'expert', split_axis=0, concat_axis=0, tiled=True)  41.6 us
    reduce_scatter x1, waiting for transfers between devices, shards(): lax.psum_scatter(gate_part, 'dp', scatter_dimension=3, tiled=True)  40.1 us
    all_to_all x1, blocking collectives, shards(): lax.all_to_all(dy_send, 'expert', split_axis=0, concat_axis=0, tiled=True)  38.4 us
    all_gather x1, waiting for transfers between devices, shards(): lax.all_gather(grad_gate_pre, 'dp', axis=3, tiled=True)  35.6 us
    all_gather x1, waiting for transfers between devices, shards(): lax.all_gather(hidden, 'dp', axis=3, tiled=True)  14.1 us
    all_gather x1, blocking collectives, shards(): lax.all_gather(block_sum, 'dp', axis=3, tiled=True)  11.9 us
    all_to_all x1, blocking collectives, shards(): lax.all_to_all(g_send, 'expert', split_axis=0, concat_axis=0, tiled=True)  10.7 us
  transfers between devices with their start and end apart: 8, of which 7 were waited for; matrix products, arithmetic and copies ran while one was open for 14% of the time, Pallas kernels for 0%

commit v1 on v0

--- a/solution.py
+++ b/solution.py
@@ -6,6 +6,19 @@
 TOP = 8
 EXPERTS = 32
 CAP = 36
+
+
+def ring_gather(x, axis, dim):
+    ways = lax.axis_size(axis)
+    up = [(d, (d + 1) % ways) for d in range(ways)]
+    down = [(d, (d - 1) % ways) for d in range(ways)]
+    earlier, later = ([x], [x])
+    for _ in range(ways // 2):
+        earlier.append(lax.ppermute(earlier[-1], axis, up))
+    for _ in range((ways - 1) // 2):
+        later.append(lax.ppermute(later[-1], axis, down))
+    line = jnp.concatenate([*earlier[::-1], *later[1:]], axis=dim)
+    return jnp.roll(line, (lax.axis_index(axis) - ways // 2) * x.shape[dim], axis=dim)
 
 
 def local_slots(expert_ids):
@@ -79,7 +92,7 @@
         lax.all_gather(hidden, "dp", axis=3, tiled=True),
         lax.all_gather(grad_gate_pre, "dp", axis=3, tiled=True),
         lax.all_gather(grad_up_pre, "dp", axis=3, tiled=True),
-        lax.all_gather(block_sum, "dp", axis=3, tiled=True),
+        ring_gather(block_sum, "dp", 3),
     )
     input_terms = jnp.einsum(
         "escf,edf->secd", gate_grad_all, gate_weight, preferred_element_type=jnp.float32

time: 408 us -> 408 us (level)
  blocking collectives: 103 us -> 90.8 us
  waiting for transfers between devices: 163 us -> 172 us
    all_gather x1 -> x0, blocking collectives: 11.9 us -> none  [shards(): lax.all_gather(block_sum, 'dp', axis=3, tiled=True)]
    ppermute x0 -> x3, waiting for transfers between devices: none -> 6 us  [the longest x2 6 us: ring_gather(): earlier.append(lax.ppermute(earlier[-1], axis, up))]
  transfers between devices with their start and end apart: 8 -> 11, of which waited for: 7 -> 9; matrix products, arithmetic and copies ran while one was open for 14% -> 14% of each run, Pallas kernels for 0% -> 0%
where the time goes in v1:
time: 408 us; the launch traced here: 407 us
  waiting for transfers between devices  172 us (42%)
  blocking collectives  90.8 us (22%)
  matrix products  56.6 us (14%)
  local copies, waits for them, and re-layouts  32.1 us (8%)
  other arithmetic  22.7 us (6%)
  starting transfers between devices  18.3 us (4%)
  between operations  14.3 us (4%)
    reduce_scatter x1, waiting for transfers between devices, shards(): lax.psum_scatter(back_part, 'dp', scatter_dimension=3, tiled=True)  57.6 us
    all_to_all x1, blocking collectives, shards(): lax.all_to_all(x_send, 'expert', split_axis=0, concat_axis=0, tiled=True)  41.6 us
    reduce_scatter x1, waiting for transfers between devices, shards(): lax.psum_scatter(gate_part, 'dp', scatter_dimension=3, tiled=True)  40.1 us
    all_to_all x1, blocking collectives, shards(): lax.all_to_all(dy_send, 'expert', split_axis=0, concat_axis=0, tiled=True)  38.4 us
    all_gather x1, waiting for transfers between devices, shards(): lax.all_gather(grad_gate_pre, 'dp', axis=3, tiled=True)  35.6 us
    all_gather x1, waiting for transfers between devices, shards(): lax.all_gather(hidden, 'dp', axis=3, tiled=True)  14.1 us
    all_to_all x1, blocking collectives, shards(): lax.all_to_all(g_send, 'expert', split_axis=0, concat_axis=0, tiled=True)  10.7 us
    another operation x2, other arithmetic  9.04 us
  transfers between devices with their start and end apart: 11, of which 9 were waited for; matrix products, arithmetic and copies ran while one was open for 14% of the time, Pallas kernels for 0%

profile of v1, /device:TPU:0, one launch (start us, length us, event | category | flops | bytes accessed | tf_op | source)
XLA Modules:
  0.0 406.6 jit_solution(2140627445903197826)
XLA Ops:
  8.4 9.0 %reduce-window.6 = s32[32,8,128]{2,1,0:T(8,128)S(1)} reduce-window(s32[32,8,128]{2,1,0:T(8,128)S(1)} %fusion.37, s32[]{:T(128)} %constant.60.clone.1), window={size=1x1x128 pad=0_0x0_0x127_0}, to_apply=%region_0.0 | reduce-window | flops 4161536 | bytes 262148 | tf_op jit(solution)/shard_map/reduce-window
  18.7 4.2 %fusion = pred[1152,128]{1,0:T(8,128)(4,1)S(1)} fusion(s32[128,8]{0,1:T(8,128)S(1)} %get-tuple-element.35), kind=kLoop, calls=%fused_computation.6 | loop fusion | flops 2211840 | bytes 151552 | tf_op jit(solution)/shard_map/reduce_or | solution.py:38
  30.1 41.6 %all_to_all.45 = bf16[32,36,1024]{2,1,0:T(8,128)(2,1)S(1)} all-to-all(bf16[32,36,1024]{2,1,0:T(8,128)(2,1)} %all_to_all.33), channel_id=1, replica_groups=mesh['expert'=32,'dp'=4] {'expert'}, dimensions={0} | all-to-all | bytes 4718592 | tf_op jit(solution)/shard_map/all_to_all | solution.py:67
  73.2 4.6 %convolution_bitcast_fusion.1 = f32[1,32,36,1024]{3,2,1,0:T(8,128)} fusion(bf16[32,36,1024]{2,1,0:T(8,128)(2,1)S(1)} %all_to_all.45, bf16[1,1024,1024]{2,1,0:T(8,128)(2,1)S(1)} %copy-done), kind=kOutput, calls=%fused_computation.21 | convolution fusion | flops 2415919104 | bytes 9175040 | tf_op jit(solution)/shard_map/secd,edf->escf/dot_general | solution.py:78
  77.9 7.6 %convolution_bitcast_fusion = f32[1,32,36,1024]{3,2,1,0:T(8,128)} fusion(bf16[32,36,1024]{2,1,0:T(8,128)(2,1)} %copy-done.2, bf16[1,1024,1024]{2,1,0:T(8,128)(2,1)} %param.11), kind=kOutput, calls=%fused_computation.20 | convolution fusion | flops 2415919104 | bytes 9175040 | tf_op jit(solution)/shard_map/secd,edf->escf/dot_general | solution.py:75
  92.8 38.4 %all_to_all.46 = bf16[32,36,1024]{2,1,0:T(8,128)(2,1)S(1)} all-to-all(bf16[32,36,1024]{2,1,0:T(8,128)(2,1)} %all_to_all.31), channel_id=1, replica_groups=mesh['expert'=32,'dp'=4] {'expert'}, dimensions={0} | all-to-all | bytes 4718592 | tf_op jit(solution)/shard_map/all_to_all | solution.py:68
  132.7 4.7 %convolution_bitcast_fusion.2 = f32[1,32,36,1024]{3,2,1,0:T(8,128)} fusion(bf16[32,36,1024]{2,1,0:T(8,128)(2,1)S(1)} %all_to_all.46, bf16[1,1024,1024]{2,1,0:T(8,128)(2,1)S(1)} %copy-done.9), kind=kOutput, calls=%fused_computation.22 | convolution fusion | flops 2415919104 | bytes 9175040 | tf_op jit(solution)/shard_map/secd,efd->escf/dot_general | solution.py:79
  139.0 10.7 %all_to_all.47 = bf16[32,36,1]{1,2,0:T(2,128)(2,1)S(1)} all-to-all(bf16[32,36,1]{1,2,0:T(2,128)(2,1)S(1)} %convert_element_type.99), channel_id=1, replica_groups=mesh['expert'=32,'dp'=4] {'expert'}, dimensions={0} | all-to-all | bytes 4608 | tf_op jit(solution)/shard_map/all_to_all | solution.py:69
  149.7 40.1 %reduce-scatter.8.cloned.1.call-done = f32[1,32,36,256]{3,2,1,0:T(8,128)} async-done(((f32[1,32,36,1024]{3,2,1,0:T(8,128)}), f32[1,32,36,256]{3,2,1,0:T(8,128)}) %reduce-scatter.8.cloned.1.call-update) | async-done | bytes 1179664 | tf_op jit(solution)/shard_map/reduce_scatter | solution.py:83
  189.9 57.6 %reduce-scatter.4.cloned.1.call-done = f32[1,32,36,256]{3,2,1,0:T(8,128)} async-done(((f32[1,32,36,1024]{3,2,1,0:T(8,128)}), f32[1,32,36,256]{3,2,1,0:T(8,128)}) %reduce-scatter.4.cloned.1.call-update) | async-done | bytes 1179664 | tf_op jit(solution)/shard_map/reduce_scatter | solution.py:85
  247.5 4.3 %multiply_reduce_fusion = (bf16[32,36]{1,0:T(8,128)(2,1)S(1)}, bf16[1,32,36,256]{3,2,1,0:T(8,128)(2,1)}, bf16[1,32,36,256]{3,2,1,0:T(8,128)(2,1)}, bf16[1,32,36,256]{3,2,1,0:T(8,128)(2,1)}) fusion(f32[1,32,36,256]{3,2,1,0:T(8,128)} %reduce-scatter.4.cloned.1.call-done, f32[1,32,36,256]{3,2,1,0:T(8,128)} %reduce-scatter.6.cloned.1.call-done, ...), kind=kLoop, calls=%fused_computation.34 | loop fusion | flops 5602176 | bytes 5315328 | tf_op jit(solution)/shard_map/reduce_sum | solution.py:90
  252.8 4.5 %collective-permute-done = bf16[1,32,36,1]{2,1,3,0:T(8,128)(2,1)S(1)} collective-permute-done((bf16[1,32,36,1]{2,1,3,0:T(8,128)(2,1)S(1)}, bf16[1,32,36,1]{2,1,3,0:T(8,128)(2,1)S(1)}, u32[]{:S(2)}, u32[]{:S(2)}) %collective-permute-start) | collective-permute-done | bytes 2336 | tf_op jit(solution)/shard_map/ppermute | solution.py:17
  262.9 7.1 %all-to-all-start.4 = ((bf16[32,36,4]{1,2,0:T(4,128)(2,1)}), bf16[32,36,4]{1,2,0:T(4,128)(2,1)S(1)}, u32[]{:S(2)}, u32[]{:S(2)}) async-start(bf16[32,36,4]{1,2,0:T(4,128)(2,1)} %copy.63), calls=%async_computation.7 | async-start | bytes 65536 | tf_op jit(solution)/shard_map/all_to_all | solution.py:119
  270.6 6.8 %all-to-all-done.4 = bf16[32,36,4]{1,2,0:T(4,128)(2,1)S(1)} async-done(((bf16[32,36,4]{1,2,0:T(4,128)(2,1)}), bf16[32,36,4]{1,2,0:T(4,128)(2,1)S(1)}, u32[]{:S(2)}, u32[]{:S(2)}) %all-to-all-start.4) | async-done | bytes 9248 | tf_op jit(solution)/shard_map/all_to_all | solution.py:119
  282.1 8.5 %all-gather.6.cloned.1.call-done = bf16[1,32,36,1024]{3,2,1,0:T(8,128)(2,1)} async-done(((bf16[1,32,36,256]{3,2,1,0:T(8,128)(2,1)}), bf16[1,32,36,1024]{3,2,1,0:T(8,128)(2,1)}) %all-gather.6.cloned.1.call-update) | async-done | bytes 2359312 | tf_op jit(solution)/shard_map/all_gather | solution.py:94
  290.6 6.4 %fusion.5 = f32[32,36,1024]{2,1,0:T(8,128)} fusion(bf16[1,32,36,1024]{3,2,1,0:T(8,128)(2,1)} %all-gather.6.cloned.1.call-done, bf16[1,1024,1024]{2,1,0:T(8,128)(2,1)S(1)} %copy-done), kind=kOutput, calls=%fused_computation.13 | convolution fusion | flops 2415919104 | bytes 9175040 | tf_op jit(solution)/shard_map/escf,edf->secd/dot_general | solution.py:100
  297.0 35.6 %all-gather.4.cloned.1.call-done = bf16[1,32,36,1024]{3,2,1,0:T(8,128)(2,1)} async-done(((bf16[1,32,36,256]{3,2,1,0:T(8,128)(2,1)}), bf16[1,32,36,1024]{3,2,1,0:T(8,128)(2,1)}) %all-gather.4.cloned.1.call-update) | async-done | bytes 2359312 | tf_op jit(solution)/shard_map/all_gather | solution.py:93
  332.6 8.3 %add_convert_fusion = bf16[32,36,1024]{2,1,0:T(8,128)(2,1)} fusion(f32[32,36,1024]{2,1,0:T(8,128)} %fusion.5, bf16[1,1024,1024]{2,1,0:T(8,128)(2,1)} %param.11, bf16[1,32,36,1024]{3,2,1,0:T(8,128)(2,1)} %all-gather.4.cloned.1.call-done), kind=kOutput, calls=%fused_computation.2 | convolution fusion | flops 2418278400 | bytes 11534336 | tf_op jit(solution)/shard_map/escf,edf->secd/dot_general | solution.py:97
  340.9 7.4 %all-to-all-start.3 = ((bf16[32,36,1024]{2,1,0:T(8,128)(2,1)}), bf16[32,36,1024]{2,1,0:T(8,128)(2,1)}, u32[]{:S(2)}, u32[]{:S(2)}) async-start(bf16[32,36,1024]{2,1,0:T(8,128)(2,1)} %add_convert_fusion), calls=%async_computation.6 | async-start | bytes 5242880 | tf_op jit(solution)/shard_map/all_to_all | solution.py:118
  348.4 7.7 %fusion.12 = f32[1,1024,1024]{2,1,0:T(8,128)} fusion(bf16[32,36,1024]{2,1,0:T(8,128)(2,1)} %copy-done.2, bf16[1,32,36,1024]{3,2,1,0:T(8,128)(2,1)} %all-gather.4.cloned.1.call-done), kind=kOutput, calls=%fused_computation.23 | convolution fusion | flops 2415919104 | bytes 8912896 | tf_op jit(solution)/shard_map/secd,escf->edf/dot_general | solution.py:110
  356.0 4.5 %fusion.15 = f32[1,1024,1024]{2,1,0:T(8,128)} fusion(bf16[32,36,1024]{2,1,0:T(8,128)(2,1)S(1)} %copy-done.3, bf16[1,32,36,1024]{3,2,1,0:T(8,128)(2,1)S(1)} %copy-done.8), kind=kOutput, calls=%fused_computation.24 | convolution fusion | flops 2415919104 | bytes 8912896 | tf_op jit(solution)/shard_map/secd,escf->edf/dot_general | solution.py:113
  360.5 14.1 %all-gather.8.cloned.1.call-done = bf16[1,32,36,1024]{3,2,1,0:T(8,128)(2,1)} async-done(((bf16[1,32,36,256]{3,2,1,0:T(8,128)(2,1)}), bf16[1,32,36,1024]{3,2,1,0:T(8,128)(2,1)}) %all-gather.8.cloned.1.call-update) | async-done | bytes 2359312 | tf_op jit(solution)/shard_map/all_gather | solution.py:92
  374.6 7.5 %fusion.18 = f32[1,1024,1024]{2,1,0:T(8,128)} fusion(bf16[32,36,1024]{2,1,0:T(8,128)(2,1)} %copy-done.4, bf16[1,32,36,1024]{3,2,1,0:T(8,128)(2,1)} %all-gather.8.cloned.1.call-done, bf16[32,36]{1,0:T(8,128)(2,1)S(1)} %get-tuple-element.37), kind=kOutput, calls=%fused_computation.25 | convolution fusion | flops 2417098752 | bytes 8915200 | tf_op jit(solution)/shard_map/escf,secd->efd/dot_general | solution.py:107
  388.3 8.1 %gather_fusion = bf16[1024,1024]{1,0:T(8,128)(2,1)} fusion(bf16[1152,1024]{1,0:T(8,128)(2,1)} %all_to_all.36, s32[1024]{0:T(1024)S(1)} %broadcast_clamp_fusion), kind=kCustom, calls=%fused_computation | custom fusion | bytes 4198400 | tf_op jit(solution)/shard_map/jit(_take)/gather | solution.py:121
  (88 shorter events, 42.8 us)
Async XLA Ops:
  7.2 66.1 %copy-start = (bf16[1,1024,1024]{2,1,0:T(8,128)(2,1)S(1)}, bf16[1,1024,1024]{2,1,0:T(8,128)(2,1)}, u32[]{:S(2)}) copy-start(bf16[1,1024,1024]{2,1,0:T(8,128)(2,1)} %param.12) | copy-start | bytes 6291460
  7.2 142.6 %reduce-scatter.6.cloned.1.call-start = ((), (), s32[]{:S(2)}) async-start(), calls=%async_computation.9 | async-start | bytes 6553600 | tf_op jit(solution)/shard_map/reduce_scatter | solution.py:84
  71.7 1.5 copy-start.2
  77.9 112.0 %reduce-scatter.8.cloned.1.call-start = ((), (), s32[]{:S(2)}) async-start(), calls=%async_computation.10 | async-start | bytes 6553600 | tf_op jit(solution)/shard_map/reduce_scatter | solution.py:83
  85.5 1.0 copy-start.5
  85.5 162.0 %reduce-scatter.4.cloned.1.call-start = ((), (), s32[]{:S(2)}) async-start(), calls=%async_computation.8 | async-start | bytes 6553600 | tf_op jit(solution)/shard_map/reduce_scatter | solution.py:85
  92.8 39.9 %copy-start.9 = (bf16[1,1024,1024]{2,1,0:T(8,128)(2,1)S(1)}, bf16[1,1024,1024]{2,1,0:T(8,128)(2,1)}, u32[]{:S(2)}) copy-start(bf16[1,1024,1024]{2,1,0:T(8,128)(2,1)} %param.13) | copy-start | bytes 6291460
  131.2 1.5 copy-start.4
  137.4 0.7 copy-start.7
  137.4 153.1 %all-gather.6.cloned.1.call-start = ((), (), s32[]{:S(2)}) async-start(), calls=%async_computation.12 | async-start | bytes 3276800 | tf_op jit(solution)/shard_map/all_gather | solution.py:94
  247.5 5.1 %copy-start.6 = (s32[128,8]{0,1:T(8,128)S(1)}, s32[128,8]{0,1:T(8,128)}, u32[]{:S(2)}) copy-start(s32[128,8]{0,1:T(8,128)} %param.10) | copy-start | bytes 12292
  251.8 80.8 %all-gather.4.cloned.1.call-start = ((), (), s32[]{:S(2)}) async-start(), calls=%async_computation.11 | async-start | bytes 3276800 | tf_op jit(solution)/shard_map/all_gather | solution.py:93
  252.4 4.9 %collective-permute-start = (bf16[1,32,36,1]{2,1,3,0:T(8,128)(2,1)S(1)}, bf16[1,32,36,1]{2,1,3,0:T(8,128)(2,1)S(1)}, u32[]{:S(2)}, u32[]{:S(2)}) collective-permute-start(bf16[1,32,36,1]{2,1,3,0:T(8,128)(2,1)S(1)} %bitcast.96), channel_id=1, source_target_pairs={{0,1},{1,2},{2,3},{3,0},{4,5},{5,6},{6,7},{7,4},{8,9},{9,10},{10,1... | collective-permute-start | bytes 6920 | tf_op jit(solution)/shard_map/ppermute | solution.py:17
  257.3 4.9 %collective-permute-start.1 = (bf16[1,32,36,1]{2,1,3,0:T(8,128)(2,1)S(1)}, bf16[1,32,36,1]{2,1,3,0:T(8,128)(2,1)S(1)}, u32[]{:S(2)}, u32[]{:S(2)}) collective-permute-start(bf16[1,32,36,1]{2,1,3,0:T(8,128)(2,1)S(1)} %collective-permute-done), channel_id=1, source_target_pairs={{0,1},{1,2},{2,3},{3,0},{4,5},{5,6},{6,7},{7,4},{8,9},{9,10},{10,1... | collective-permute-start | bytes 6920 | tf_op jit(solution)/shard_map/ppermute | solution.py:17
  257.4 4.8 %collective-permute-start.2 = (bf16[1,32,36,1]{2,1,3,0:T(8,128)(2,1)S(1)}, bf16[1,32,36,1]{2,1,3,0:T(8,128)(2,1)S(1)}, u32[]{:S(2)}, u32[]{:S(2)}) collective-permute-start(bf16[1,32,36,1]{2,1,3,0:T(8,128)(2,1)S(1)} %bitcast.97), channel_id=1, source_target_pairs={{0,3},{1,0},{2,1},{3,2},{4,7},{5,4},{6,5},{7,6},{8,11},{9,8},{10,9... | collective-permute-start | bytes 6920 | tf_op jit(solution)/shard_map/ppermute | solution.py:19
  262.9 14.5 %all-to-all-start.4 = ((bf16[32,36,4]{1,2,0:T(4,128)(2,1)}), bf16[32,36,4]{1,2,0:T(4,128)(2,1)S(1)}, u32[]{:S(2)}, u32[]{:S(2)}) async-start(bf16[32,36,4]{1,2,0:T(4,128)(2,1)} %copy.63), calls=%async_computation.7 | async-start | bytes 65536 | tf_op jit(solution)/shard_map/all_to_all | solution.py:119
  270.0 104.6 %all-gather.8.cloned.1.call-start = ((), (), s32[]{:S(2)}) async-start(), calls=%async_computation.13 | async-start | bytes 3276800 | tf_op jit(solution)/shard_map/all_gather | solution.py:92
  340.9 43.3 %all-to-all-start.3 = ((bf16[32,36,1024]{2,1,0:T(8,128)(2,1)}), bf16[32,36,1024]{2,1,0:T(8,128)(2,1)}, u32[]{:S(2)}, u32[]{:S(2)}) async-start(bf16[32,36,1024]{2,1,0:T(8,128)(2,1)} %add_convert_fusion), calls=%async_computation.6 | async-start | bytes 5242880 | tf_op jit(solution)/shard_map/all_to_all | solution.py:118
  348.4 7.7 %copy-start.3 = (bf16[32,36,1024]{2,1,0:T(8,128)(2,1)S(1)}, bf16[32,36,1024]{2,1,0:T(8,128)(2,1)}, u32[]{:S(2)}) copy-start(bf16[32,36,1024]{2,1,0:T(8,128)(2,1)} %copy-done.2) | copy-start | bytes 7077892
  348.4 7.7 %copy-start.8 = (bf16[1,32,36,1024]{3,2,1,0:T(8,128)(2,1)S(1)}, bf16[1,32,36,1024]{3,2,1,0:T(8,128)(2,1)}, u32[]{:S(2)}) copy-start(bf16[1,32,36,1024]{3,2,1,0:T(8,128)(2,1)} %all-gather.6.cloned.1.call-done) | copy-start | bytes 7077892
  388.3 11.5 %copy-start.1 = (bf16[1,1024,1024]{2,1,0:T(8,128)(2,1)S(1)}, bf16[1,1024,1024]{2,1,0:T(8,128)(2,1)}, u32[]{:S(2)}) copy-start(bf16[1,1024,1024]{2,1,0:T(8,128)(2,1)} %param.12) | copy-start | bytes 6291460
Sparse Core Ops, SparseCore 0:
  78.0 54.2 reduce-scatter.5
  134.7 55.1 reduce-scatter.7
  192.3 55.1 reduce-scatter.3
  251.9 38.6 all-gather.5
  292.7 39.8 all-gather.3
  334.7 39.8 all-gather.7
